TPU v7x, 128 devices: a whole 4x4x4 slice. The times are simulated.
128 devices in a mesh: ctx: 32 (over x, z, core), fsdp: 4 (over y).
Axes of the slice: x: 4, y: 4, z: 4, core: 2. Of those that a mesh axis runs over, the one named last changes fastest.
Arguments:
- tokens: bfloat16 [4, 8192, 8192], P('fsdp', 'ctx'), may hold values from -6 to 6
- queries: bfloat16 [4, 8192, 8192], P('fsdp', 'ctx'), may hold values from -384 to 384
- kv_weight: bfloat16 [8192, 2048], P(None, 'fsdp'), may hold values from -0.0625 to 0.0625
- block_list: int32 [8, 64, 8], replicated, may hold values from 0 to 63, as said below
- counts: int32 [8, 64], replicated, may hold values from 4 to 8, as said below
Outputs:
- attended: bfloat16 [4, 8192, 8192], P('fsdp', 'ctx')
Inputs may be any that keep to these rules, and one draw needn't show every extreme that they name: `block_list`: for each g and b the first counts[g, b] entries are distinct: block b, blocks b - 1 and b + 1 modulo 64 (the window wraps at the sequence's ends), the two global blocks of group g, and random blocks; the later entries are further distinct blocks. `counts`: some list has 8 live entries in every draw; loads differ from group to group.
All inputs are finite; a program needn't handle non-finite values.
Results may differ from a plain program's by a relative error of at most 0.007.
The roundings to bfloat16 on the way count: a program that leaves them out, or rounds other values in their place, can miss the bound.
Values may be sent and summed in bfloat16 or wider, within the bound.
A program may use at most 192 MiB of HBM per device.

v0:
```python
import jax
import jax.numpy as jnp
from jax import lax
from jax.sharding import PartitionSpec as P

HQ = 64
KVH = 8
DH = 128
BLK = 128


def on_device(tokens, queries, kv_weight, block_list, counts):
    seq_rows = tokens.shape[1]
    n_ctx = lax.axis_size("ctx")
    kv_width = kv_weight.shape[1] * lax.axis_size("fsdp")
    pair_width = 2 * DH
    kv_heads = kv_width // pair_width
    copies = n_ctx // kv_heads
    column_part = jnp.einsum(
        "std,dc->stc",
        lax.all_gather(tokens, "fsdp", axis=0, tiled=True),
        kv_weight,
        preferred_element_type=jnp.float32,
    ).astype(jnp.bfloat16)
    keyvals = lax.all_to_all(column_part, "fsdp", split_axis=0, concat_axis=2, tiled=True)
    spread = jnp.broadcast_to(
        keyvals.reshape(1, seq_rows, kv_heads, 1, pair_width),
        (1, seq_rows, kv_heads, copies, pair_width),
    )
    spread = spread.reshape(1, seq_rows, kv_heads * copies * pair_width)
    query_local, keyval_local = (
        lax.all_to_all(queries, "ctx", split_axis=2, concat_axis=1, tiled=True),
        lax.all_to_all(spread, "ctx", split_axis=2, concat_axis=1, tiled=True),
    )
    head_count = query_local.shape[2] // DH
    length = query_local.shape[1]
    blocks = length // BLK
    kv_group = lax.axis_index("ctx") * head_count // (HQ // KVH)
    my_list = lax.dynamic_index_in_dim(block_list, kv_group, 0, keepdims=False)
    my_counts = lax.dynamic_index_in_dim(counts, kv_group, 0, keepdims=False)
    query_blocks = query_local.reshape(blocks, BLK, head_count, DH)
    keyval_blocks = keyval_local.reshape(blocks, BLK, pair_width)
    score_scale = DH ** (-0.5)
    slot_trips = jnp.max(my_counts)

    def slot_step(slot, state):
        row_top, row_total, weighted = state
        chosen = jnp.take(keyval_blocks, my_list[:, slot], axis=0)
        key_rows = chosen[:, :, :DH]
        value_rows = chosen[:, :, DH:]
        scores = (
            jnp.einsum("nqhd,nkd->nqhk", query_blocks, key_rows, preferred_element_type=jnp.float32)
            * score_scale
        )
        live_slot = (slot < my_counts)[:, None, None, None]
        scores = jnp.where(live_slot, scores, -jnp.inf)
        new_top = jnp.maximum(row_top, jnp.max(scores, axis=3))
        rescale = jnp.exp(row_top - new_top)
        weights = jnp.exp(scores - new_top[..., None])
        row_total = row_total * rescale + jnp.sum(weights, axis=3)
        update = jnp.einsum(
            "nqhk,nkd->nqhd",
            weights.astype(jnp.bfloat16),
            value_rows,
            preferred_element_type=jnp.float32,
        )
        weighted = weighted * rescale[..., None] + update
        return (new_top, row_total, weighted)

    start_state = (
        jnp.full((blocks, BLK, head_count), -jnp.inf, jnp.float32),
        jnp.zeros((blocks, BLK, head_count), jnp.float32),
        jnp.zeros((blocks, BLK, head_count, DH), jnp.float32),
    )
    row_top, row_total, weighted = lax.fori_loop(0, slot_trips, slot_step, start_state)
    result = (
        (weighted / row_total[..., None]).astype(jnp.bfloat16).reshape(1, length, head_count * DH)
    )
    return lax.all_to_all(result, "ctx", split_axis=1, concat_axis=2, tiled=True)


def solution(mesh):
    return jax.shard_map(
        on_device,
        mesh=mesh,
        in_specs=(P("fsdp", "ctx", None), P("fsdp", "ctx", None), P(None, "fsdp"), P(), P()),
        out_specs=P("fsdp", "ctx", None),
        check_vma=False,
    )
```

profile of v0, /device:TPU:24, one launch (start us, length us, event | category | flops | bytes accessed | tf_op | source)
XLA Modules:
  0.0 840.4 jit_solution(7300504675332604300)
XLA Ops:
  7.3 156.8 %all-gather.2.cloned.1.call-done = bf16[4,256,8192]{2,1,0:T(8,128)(2,1)} async-done(((bf16[1,256,8192]{2,1,0:T(8,128)(2,1)}), bf16[4,256,8192]{2,1,0:T(8,128)(2,1)}) %all-gather.2.cloned.1.call-update) | async-done | bytes 16777232 | tf_op jit(solution)/shard_map/all_gather | solution.py:21
  164.0 15.6 %fusion.16 = bf16[4,256,512]{2,1,0:T(8,128)(2,1)} fusion(bf16[4,256,8192]{2,1,0:T(8,128)(2,1)} %all-gather.2.cloned.1.call-done, bf16[8192,512]{1,0:T(8,128)(2,1)} %param.9), kind=kOutput, calls=%fused_computation.28 | convolution fusion | flops 8590458880 | bytes 26214400 | tf_op jit(solution)/shard_map/std,dc->stc/dot_general | solution.py:19
  185.3 17.8 %copy.36 = bf16[1,256,8192]{1,0,2:T(2,128)(2,1)} copy(bf16[1,256,8192]{2,1,0:T(8,128)(2,1)} %param.8) | data formatting | bytes 8388608 | tf_op args[1]
  203.7 43.5 %reduce.2 = bf16[8192,256]{1,0:T(8,128)(2,1)} reduce(bf16[8192,1,256]{2,1,0:T(2,128)(2,1)} %bitcast.102, bf16[]{:T(256)} %broadcast.39), dimensions={1}, to_apply=%bitcast.56.reduce_sub_computation | reduce | bytes 8388610
  254.1 7.8 all-to-all-start.2
  262.9 49.5 %copy.52 = bf16[1,256,8192]{1,0,2:T(2,128)(2,1)} copy(bf16[1,256,8192]{1,2,0:T(8,128)(2,1)S(1)} %bitcast.108) | data formatting | bytes 8388608 | tf_op jit(solution)/shard_map/broadcast_in_dim | solution.py:26
  312.4 43.5 %reduce.1 = bf16[8192,256]{1,0:T(8,128)(2,1)} reduce(bf16[8192,1,256]{2,1,0:T(2,128)(2,1)} %bitcast.104, bf16[]{:T(256)} %broadcast.39), dimensions={1}, to_apply=%bitcast.65.reduce_sub_computation | reduce | bytes 8388610
  362.9 7.8 all-to-all-start.1
  372.0 19.8 %reshape.48 = bf16[8192,1,256]{2,1,0:T(2,128)(2,1)} reshape(bf16[32,2,32768]{2,1,0:T(2,128)(2,1)} %all-to-all-done.2) | data formatting | bytes 8388608
  400.4 7.1 reshape.31
  414.3 9.1 %all-to-all-done.1 = bf16[32,2,32768]{2,1,0:T(2,128)(2,1)} async-done(((bf16[32,2,32768]{2,1,0:T(2,128)(2,1)}), bf16[32,2,32768]{2,1,0:T(2,128)(2,1)}, u32[]{:S(2)}, u32[]{:S(2)}) %all-to-all-start.1) | async-done | bytes 4194336 | tf_op jit(solution)/shard_map/all_to_all | solution.py:33
  423.4 19.8 %reshape.46 = bf16[8192,1,256]{2,1,0:T(2,128)(2,1)} reshape(bf16[32,2,32768]{2,1,0:T(2,128)(2,1)} %all-to-all-done.1) | data formatting | bytes 8388608
  460.0 166.0 %while.14 = (s32[]{:T(128)}, f32[64,128,2]{1,2,0:T(2,128)S(1)}, f32[64,128,2]{1,2,0:T(2,128)S(1)}, f32[64,128,2,128]{3,1,2,0:T(8,128)}, s32[]{:T(128)}, /*index=...) while((s32[]{:T(128)}, f32[64,128,2]{1,2,0:T(2,128)S(1)}, ...), condition=%wide.region_4.5_spmd, body=%wide.region_1.4_spmd.sunk | while | flops 1103136256 | bytes 84941504 | solution.py:75
  473.4 10.1 %multiply_add_fusion.5 = f32[64,128,2,128]{3,1,2,0:T(8,128)} fusion(f32[64,128,2,128]{3,1,2,0:T(8,128)} %get-tuple-element.205, f32[64,128,2]{1,2,0:T(2,128)S(1)} %bitcast.114, f32[64,128,128,2]{2,1,3,0:T(8,128)S(1)} %get-tuple-element.187, f32[64,128,2]{1,2,0:T(2,128)S(1)} %max.4, pred[64]{0:T(512)(128)(4,1)S(1)} %broadcast_compare_fusion.2, ...), kind=kOutput, calls=%fused_computation.4.clone.1 | convolution fusion | flops 549453824 | bytes 27394560 | tf_op jit(solution)/shard_map/while/body/nqhk,nkd->nqhd/dot_general | solution.py:61
  497.0 10.1 %multiply_add_fusion.5 = f32[64,128,2,128]{3,1,2,0:T(8,128)} fusion(f32[64,128,2,128]{3,1,2,0:T(8,128)} %get-tuple-element.205, f32[64,128,2]{1,2,0:T(2,128)S(1)} %bitcast.114, f32[64,128,128,2]{2,1,3,0:T(8,128)S(1)} %get-tuple-element.187, f32[64,128,2]{1,2,0:T(2,128)S(1)} %max.4, pred[64]{0:T(512)(128)(4,1)S(1)} %broadcast_compare_fusion.2, ...), kind=kOutput, calls=%fused_computation.4.clone.1 | convolution fusion | flops 549453824 | bytes 27394560 | tf_op jit(solution)/shard_map/while/body/nqhk,nkd->nqhd/dot_general | solution.py:61
  520.6 10.1 %multiply_add_fusion.5 = f32[64,128,2,128]{3,1,2,0:T(8,128)} fusion(f32[64,128,2,128]{3,1,2,0:T(8,128)} %get-tuple-element.205, f32[64,128,2]{1,2,0:T(2,128)S(1)} %bitcast.114, f32[64,128,128,2]{2,1,3,0:T(8,128)S(1)} %get-tuple-element.187, f32[64,128,2]{1,2,0:T(2,128)S(1)} %max.4, pred[64]{0:T(512)(128)(4,1)S(1)} %broadcast_compare_fusion.2, ...), kind=kOutput, calls=%fused_computation.4.clone.1 | convolution fusion | flops 549453824 | bytes 27394560 | tf_op jit(solution)/shard_map/while/body/nqhk,nkd->nqhd/dot_general | solution.py:61
  544.2 10.1 %multiply_add_fusion.5 = f32[64,128,2,128]{3,1,2,0:T(8,128)} fusion(f32[64,128,2,128]{3,1,2,0:T(8,128)} %get-tuple-element.205, f32[64,128,2]{1,2,0:T(2,128)S(1)} %bitcast.114, f32[64,128,128,2]{2,1,3,0:T(8,128)S(1)} %get-tuple-element.187, f32[64,128,2]{1,2,0:T(2,128)S(1)} %max.4, pred[64]{0:T(512)(128)(4,1)S(1)} %broadcast_compare_fusion.2, ...), kind=kOutput, calls=%fused_computation.4.clone.1 | convolution fusion | flops 549453824 | bytes 27394560 | tf_op jit(solution)/shard_map/while/body/nqhk,nkd->nqhd/dot_general | solution.py:61
  567.8 10.1 %multiply_add_fusion.5 = f32[64,128,2,128]{3,1,2,0:T(8,128)} fusion(f32[64,128,2,128]{3,1,2,0:T(8,128)} %get-tuple-element.205, f32[64,128,2]{1,2,0:T(2,128)S(1)} %bitcast.114, f32[64,128,128,2]{2,1,3,0:T(8,128)S(1)} %get-tuple-element.187, f32[64,128,2]{1,2,0:T(2,128)S(1)} %max.4, pred[64]{0:T(512)(128)(4,1)S(1)} %broadcast_compare_fusion.2, ...), kind=kOutput, calls=%fused_computation.4.clone.1 | convolution fusion | flops 549453824 | bytes 27394560 | tf_op jit(solution)/shard_map/while/body/nqhk,nkd->nqhd/dot_general | solution.py:61
  591.4 10.1 %multiply_add_fusion.5 = f32[64,128,2,128]{3,1,2,0:T(8,128)} fusion(f32[64,128,2,128]{3,1,2,0:T(8,128)} %get-tuple-element.205, f32[64,128,2]{1,2,0:T(2,128)S(1)} %bitcast.114, f32[64,128,128,2]{2,1,3,0:T(8,128)S(1)} %get-tuple-element.187, f32[64,128,2]{1,2,0:T(2,128)S(1)} %max.4, pred[64]{0:T(512)(128)(4,1)S(1)} %broadcast_compare_fusion.2, ...), kind=kOutput, calls=%fused_computation.4.clone.1 | convolution fusion | flops 549453824 | bytes 27394560 | tf_op jit(solution)/shard_map/while/body/nqhk,nkd->nqhd/dot_general | solution.py:61
  615.0 10.1 %multiply_add_fusion.5 = f32[64,128,2,128]{3,1,2,0:T(8,128)} fusion(f32[64,128,2,128]{3,1,2,0:T(8,128)} %get-tuple-element.205, f32[64,128,2]{1,2,0:T(2,128)S(1)} %bitcast.114, f32[64,128,128,2]{2,1,3,0:T(8,128)S(1)} %get-tuple-element.187, f32[64,128,2]{1,2,0:T(2,128)S(1)} %max.4, pred[64]{0:T(512)(128)(4,1)S(1)} %broadcast_compare_fusion.2, ...), kind=kOutput, calls=%fused_computation.4.clone.1 | convolution fusion | flops 549453824 | bytes 27394560 | tf_op jit(solution)/shard_map/while/body/nqhk,nkd->nqhd/dot_general | solution.py:61
  637.6 25.9 %reshape.44 = bf16[1,8192,256]{2,0,1:T(2,128)(2,1)} reshape(bf16[64,128,2,128]{3,2,1,0:T(2,128)(2,1)} %copy.46) | data formatting | bytes 8388608 | tf_op jit(solution)/shard_map/reshape | solution.py:77
  663.5 43.5 %reduce.3 = bf16[8192,256]{1,0:T(8,128)(2,1)} reduce(bf16[8192,1,256]{2,1,0:T(2,128)(2,1)} %bitcast.103, bf16[]{:T(256)} %broadcast.39), dimensions={1}, to_apply=%bitcast.58.reduce_sub_computation | reduce | bytes 8388610
  713.9 80.7 %all_to_all.63 = bf16[32,2,32768]{2,1,0:T(2,128)(2,1)} all-to-all(bf16[32,2,32768]{2,1,0:T(2,128)(2,1)} %reshape.49), channel_id=1, replica_groups=mesh['ctx'=32,'fsdp'=4] {'ctx'}, dimensions={0} | all-to-all | bytes 8388608 | tf_op jit(solution)/shard_map/all_to_all | solution.py:79
  794.7 19.8 %reshape.50 = bf16[8192,1,256]{2,1,0:T(2,128)(2,1)} reshape(bf16[32,2,32768]{2,1,0:T(2,128)(2,1)} %all_to_all.63) | data formatting | bytes 8388608
  (114 shorter events, 182.0 us)
Async XLA Ops:
  6.5 365.5 %copy-start = (s32[8,64,8]{1,2,0:T(8,128)S(1)}, s32[8,64,8]{1,2,0:T(8,128)}, u32[]{:S(2)}) copy-start(s32[8,64,8]{1,2,0:T(8,128)} %param.10) | copy-start | bytes 49156
  6.5 157.5 %all-gather.2.cloned.1.call-start = ((), (), s32[]{:S(2)}) async-start(), calls=%async_computation.4 | async-start | bytes 20971520 | tf_op jit(solution)/shard_map/all_gather | solution.py:21
  179.6 74.5 %all-to-all-start = ((bf16[4,256,512]{2,1,0:T(8,128)(2,1)}), bf16[4,256,512]{2,1,0:T(8,128)(2,1)S(1)}, u32[]{:S(2)}, u32[]{:S(2)}) async-start(bf16[4,256,512]{2,1,0:T(8,128)(2,1)} %fusion.16), calls=%async_computation | async-start | bytes 2097152 | tf_op jit(solution)/shard_map/all_to_all | solution.py:25
  254.1 108.8 %all-to-all-start.2 = ((bf16[32,2,32768]{2,1,0:T(2,128)(2,1)}), bf16[32,2,32768]{2,1,0:T(2,128)(2,1)}, u32[]{:S(2)}, u32[]{:S(2)}) async-start(bf16[32,2,32768]{2,1,0:T(2,128)(2,1)} %reshape.47), calls=%async_computation.2 | async-start | bytes 8388608 | tf_op jit(solution)/shard_map/all_to_all | solution.py:32
  362.9 60.5 %all-to-all-start.1 = ((bf16[32,2,32768]{2,1,0:T(2,128)(2,1)}), bf16[32,2,32768]{2,1,0:T(2,128)(2,1)}, u32[]{:S(2)}, u32[]{:S(2)}) async-start(bf16[32,2,32768]{2,1,0:T(2,128)(2,1)} %reshape.45), calls=%async_computation.1 | async-start | bytes 8388608 | tf_op jit(solution)/shard_map/all_to_all | solution.py:33
  465.7 3.4 copy-start.2
  489.3 3.4 copy-start.2
  512.9 3.4 copy-start.2
  536.5 3.4 copy-start.2
  560.1 3.4 copy-start.2
  583.7 3.4 copy-start.2
  607.3 3.4 copy-start.2
  827.0 6.3 copy-start.1
Sparse Core Ops, SparseCore 0:
  9.0 154.9 all-gather.1
where the time goes:
time: 852 us; the launch traced here: 840 us
  local copies, waits for them, and re-layouts  279 us (33%)
  other arithmetic  175 us (21%)
  waiting for transfers between devices  167 us (20%)
  matrix products  97.9 us (11%)
  blocking collectives  80.7 us (9%)
  starting transfers between devices  21.3 us (2%)
  between operations  13.7 us (2%)
    all_gather x1, waiting for transfers between devices, on_device(): lax.all_gather(tokens, 'fsdp', axis=0, tiled=True)  157 us
    unnamed x3, other arithmetic  131 us
    unnamed x15, local copies, waits for them, and re-layouts  115 us
    all_to_all x1, blocking collectives, on_device(): lax.all_to_all(result, 'ctx', split_axis=1, concat_axis=2, tiled=True)  80.7 us
    dot_general x7, matrix products, slot_step(): jnp.einsum('nqhk,nkd->nqhd', weights.astype(jnp.bfloat16), value_rows, pr...  71 us
    broadcast_in_dim x2, local copies, waits for them, and re-layouts, on_device(): jnp.broadcast_to(keyvals.reshape(1, seq_rows, kv_heads, 1, pair_width), (...  50 us
    gather x7, local copies, waits for them, and re-layouts, slot_step(): chosen = jnp.take(keyval_blocks, my_list[:, slot], axis=0)  35.1 us
    reshape x2, local copies, waits for them, and re-layouts, on_device(): (weighted / row_total[..., None]).astype(jnp.bfloat16)  32.3 us
  transfers between devices with their start and end apart: 4, of which 2 were waited for; matrix products, arithmetic and copies ran while one was open for 25% of the time, Pallas kernels for 0%

commit v1 on v0

v1 whole, which is shorter than its diff:
```python
import functools

import jax
import jax.numpy as jnp
from jax import lax
from jax.experimental import pallas as pl
from jax.experimental.pallas import tpu as pltpu
from jax.sharding import Mesh
from jax.sharding import PartitionSpec as P

HQ = 64
KVH = 8
DH = 128
BLK = 128
MAXK = 8
GROUP = HQ // KVH
PAIR = 2 * DH
COLS = GROUP * DH
ROWS = GROUP * BLK
RING = 4
HALF = 256
PIECE = 512
MESH_ID = pl.DeviceIdType.MESH
BF16 = jnp.bfloat16
OWN, FAR_W, NEAR_K, FAR, NEAR_V = range(5)
LOG2E = 1.4426950408889634


def fused_kernel(
    first, second, third, bias, tokens, queries, w, out,
    tok, q, w_own, w_nk, w_nv, g0, g1, g2, g3, g4, s_buf, p_buf, v_buf, ob,
    local_sem, far_send, far_recv, tok_send, tok_recv, q_send, q_recv,
    w_send, w_recv, ag_send, ag_recv, o_local, o_send, o_recv,
):
    g = [g0, g1, g2, g3, g4]
    x, z, c, y = (lax.axis_index(n) for n in ("x", "z", "c", "y"))
    a = x + c * (z - x)
    b = z + c * (x - z)
    mod = lambda v: lax.rem(v + RING, RING)
    ap, am, bp, bm = mod(a + 1), mod(a - 1), mod(b + 1), mod(b - 1)
    plane = lambda a_, b_: (a_ + c * (b_ - a_), b_ + c * (a_ - b_), c, y)
    to_ap, to_am, to_bp, to_bm = plane(ap, b), plane(am, b), plane(a, bp), plane(a, bm)
    up, down, far = (x, z, c, mod(y + 1)), (x, z, c, mod(y - 1)), (x, z, c, mod(y + 2))
    mate = (x, z, 1 - c, y)
    everyone = [to_ap, to_am, to_bp, to_bm, up, down, far, mate]
    my_cols = pl.multiple_of(c * PAIR, PAIR)
    q_col = lambda h, core: pl.ds(pl.multiple_of((mod(y + h) * 2 + core) * COLS, COLS), COLS)

    def remote(src, dst, send, recv, dev):
        return pltpu.make_async_remote_copy(
            src_ref=src, dst_ref=dst, send_sem=send, recv_sem=recv,
            device_id=dev, device_id_type=MESH_ID,
        )

    own_copies = [
        pltpu.make_async_copy(tokens, tok.at[c], local_sem.at[0]),
        pltpu.make_async_copy(w.at[:, :, pl.ds(my_cols, PAIR)], w_own, local_sem.at[1]),
    ]
    q_copies = [
        pltpu.make_async_copy(queries.at[:, q_col(h, c)], q.at[h, c], local_sem.at[2 + h])
        for h in range(RING)
    ]
    for copy in own_copies + q_copies:
        copy.start()
    v_buf[:, DH:] = jnp.ones((MAXK * BLK, DH), BF16)

    barrier = pltpu.get_barrier_semaphore()
    for dev in everyone:
        pl.semaphore_signal(barrier, inc=1, device_id=dev, device_id_type=MESH_ID)
    pl.semaphore_wait(barrier, len(everyone))

    far_copy = remote(
        w.at[pl.ds((a * RING + b) * RING, RING), :, pl.ds(my_cols, PAIR)], g[FAR_W].at[a, b], far_send, far_recv, far
    )
    tok_copy = remote(tokens, tok.at[c], tok_send, tok_recv, mate)
    k_cols = w.at[:, :, pl.ds(my_cols, DH)]
    v_cols = w.at[:, :, pl.ds(pl.multiple_of(my_cols + DH, DH), DH)]
    w_copies = [
        remote(k_cols, w_nk.at[:, :, DH:], w_send.at[0], w_recv.at[0], up),
        remote(k_cols, w_nk.at[:, :, :DH], w_send.at[1], w_recv.at[1], down),
        remote(v_cols, w_nv.at[:, :, DH:], w_send.at[2], w_recv.at[2], up),
        remote(v_cols, w_nv.at[:, :, :DH], w_send.at[3], w_recv.at[3], down),
    ]
    q_moves = [
        remote(queries.at[:, q_col(h, 1 - c)], q.at[h, c], q_send.at[h], q_recv.at[h], mate)
        for h in range(RING)
    ]
    for copy in [far_copy, tok_copy] + w_copies + q_moves:
        copy.start()

    def move(u, k):
        src, dev = [
            (g[u].at[a, b], to_ap),
            (g[u].at[a, b], to_am),
            (g[u].at[am, b, pl.ds(0, 2)], to_ap),
            (g[u].at[ap, b, pl.ds(2, 2)], to_am),
            (g[u].at[:, b], to_bp),
            (g[u].at[:, b], to_bm),
            (g[u].at[:, bm, pl.ds(0, 2)], to_bp),
            (g[u].at[:, bp, pl.ds(2, 2)], to_bm),
        ][k]
        return remote(src, src, ag_send.at[u, k], ag_recv.at[u, k], dev)

    def s0(u):
        move(u, 0).start()
        move(u, 1).start()

    def s1(u):
        move(u, 0).wait_recv()
        move(u, 2).start()
        move(u, 1).wait_recv()
        move(u, 3).start()

    def s2(u):
        move(u, 2).wait_recv()
        move(u, 3).wait_recv()
        move(u, 4).start()
        move(u, 5).start()

    def s3(u):
        move(u, 4).wait_recv()
        move(u, 6).start()
        move(u, 5).wait_recv()
        move(u, 7).start()

    def s4(u):
        move(u, 6).wait_recv()
        move(u, 7).wait_recv()

    def project(u, owner, weight):
        rows = jnp.dot(tok[owner], weight[...].reshape(-1, PAIR), preferred_element_type=jnp.float32)
        g[u][a, b, pl.ds(owner * 2, 2)] = rows.astype(BF16).reshape(2, BLK, PAIR)

    def project_both(u, weight):
        @pl.loop(0, 2)
        def _(i):
            project(u, i, weight)

    sources = [
        (OWN, 0, OWN, DH),
        (NEAR_K, 0, NEAR_V, 0),
        (FAR, 0, FAR, DH),
        (NEAR_K, DH, NEAR_V, DH),
    ]

    def attend(h, mine, i):
        owner = c if mine else 1 - c
        group = mod(y + h) * 2 + c
        block = (x * RING + z) * 4 + owner * 2 + i
        entry = (group * 64 + block) * MAXK
        ku, kc, vu, vc = sources[h]
        q_rows = q[h, owner, pl.ds(pl.multiple_of(i * BLK, BLK), BLK), :]
        q_all = jnp.concatenate([q_rows[:, n * DH : (n + 1) * DH] for n in range(GROUP)], axis=0)
        top = None
        for j in range(MAXK):
            ka, kbb, kr = first[entry + j], second[entry + j], third[entry + j]
            k_rows = g[ku][ka, kbb, kr, :, kc : kc + DH]
            v_rows = g[vu][ka, kbb, kr, :, vc : vc + DH]
            v_buf[j * BLK : (j + 1) * BLK, :DH] = v_rows
            scores = lax.dot_general(
                q_all, k_rows, (((1,), (1,)), ((), ())), preferred_element_type=jnp.float32
            )
            if j >= 4:
                scores = scores + bias[entry + j]
            s_buf[:, j * BLK : (j + 1) * BLK] = scores
            top = scores if top is None else jnp.maximum(top, scores)
        row_top = jnp.max(top, axis=1, keepdims=True)
        for j in range(MAXK):
            weights = jnp.exp2((s_buf[:, j * BLK : (j + 1) * BLK] - row_top) * (DH ** (-0.5) * LOG2E))
            p_buf[:, j * BLK : (j + 1) * BLK] = weights.astype(BF16)
        mixed = jnp.dot(p_buf[...], v_buf[...], preferred_element_type=jnp.float32)
        res = (mixed[:, :DH] / mixed[:, DH:]).astype(BF16)
        slot = (0 if mine else 2) + i
        for n in range(GROUP):
            ob[h, slot, :, n * DH : (n + 1) * DH] = res[n * BLK : (n + 1) * BLK, :]

    def result(h, mine, i):
        at = out.at[pl.ds(pl.multiple_of(i * BLK, BLK), BLK), q_col(h, c)]
        if mine:
            return pltpu.make_async_copy(ob.at[h, i], at, o_local.at[h, i])
        return remote(ob.at[h, 2 + i], at, o_send.at[h, i], o_recv.at[h, i], mate)

    def head(h, mine):
        @pl.loop(0, 2)
        def _(i):
            attend(h, mine, i)
            result(h, mine, i).start()

    for copy in own_copies:
        copy.wait()
    project(OWN, c, w_own)
    far_copy.wait_recv()
    s0(FAR_W)
    tok_copy.wait_recv()
    project(OWN, 1 - c, w_own)
    s0(OWN)
    s1(FAR_W)
    s1(OWN)
    s2(FAR_W)
    s2(OWN)
    s3(FAR_W)
    s3(OWN)
    s4(FAR_W)
    project_both(FAR, g[FAR_W])
    s0(FAR)
    s4(OWN)
    w_copies[0].wait_recv()
    w_copies[1].wait_recv()
    project_both(NEAR_K, w_nk)
    s0(NEAR_K)
    s1(FAR)
    s1(NEAR_K)
    s2(FAR)
    for copy in q_copies:
        copy.wait()
    for copy in q_moves:
        copy.wait_recv()
    head(0, False)
    s2(NEAR_K)
    s3(FAR)
    head(0, True)
    s4(FAR)
    s3(NEAR_K)
    head(2, False)
    s4(NEAR_K)
    w_copies[2].wait_recv()
    w_copies[3].wait_recv()
    project_both(NEAR_V, w_nv)
    s0(NEAR_V)
    s1(NEAR_V)
    s2(NEAR_V)
    head(2, True)
    s3(NEAR_V)
    s4(NEAR_V)
    head(1, False)
    head(3, False)
    head(1, True)
    head(3, True)

    far_copy.wait_send()
    tok_copy.wait_send()
    for copy in w_copies + q_moves:
        copy.wait_send()
    for u in range(5):
        for k in range(8):
            move(u, k).wait_send()
    for h in range(RING):
        for i in range(2):
            result(h, True, i).wait()
            result(h, False, i).wait()


def fused(tables, bias, tokens, queries, w):
    dma = pltpu.SemaphoreType.DMA
    anywhere = pl.BlockSpec(memory_space=pl.ANY)
    smem = pl.BlockSpec(memory_space=pltpu.SMEM)
    rows, depth = tokens.shape
    return pl.pallas_call(
        fused_kernel,
        out_shape=jax.ShapeDtypeStruct(queries.shape, BF16),
        in_specs=[smem, smem, smem, smem, anywhere, anywhere, anywhere],
        out_specs=anywhere,
        scratch_shapes=[
            pltpu.VMEM((2, rows, depth), BF16),
            pltpu.VMEM((RING, 2, rows, COLS), BF16),
            pltpu.VMEM((depth // BLK, BLK, PAIR), BF16),
            pltpu.VMEM((depth // BLK, BLK, PAIR), BF16),
            pltpu.VMEM((depth // BLK, BLK, PAIR), BF16),
            *[pltpu.VMEM((RING, RING, RING, BLK, PAIR), BF16) for _ in range(5)],
            pltpu.VMEM((ROWS, MAXK * BLK), jnp.float32),
            pltpu.VMEM((ROWS, MAXK * BLK), BF16),
            pltpu.VMEM((MAXK * BLK, PAIR), BF16),
            pltpu.VMEM((RING, 4, BLK, COLS), BF16),
            dma((6,)), dma, dma, dma, dma, dma((4,)), dma((4,)),
            dma((4,)), dma((4,)), dma((5, 8)), dma((5, 8)),
            dma((RING, 2)), dma((RING, 2)), dma((RING, 2)),
        ],
        compiler_params=pltpu.CompilerParams(
            collective_id=0, has_side_effects=True, vmem_limit_bytes=67043328
        ),
        name="fused",
    )(*tables, bias, tokens, queries, w)


def on_device(tokens, queries, kv_weight, block_list, counts):
    c = lax.axis_index("c")
    chip, row = block_list // 4, block_list % 4
    kx, kz = chip // RING, chip % RING
    tables = (jnp.where(c == 0, kx, kz), jnp.where(c == 0, kz, kx), row)
    bias = jnp.where(jnp.arange(MAXK) < counts[..., None], 0.0, -1e30).astype(jnp.float32)
    weight = kv_weight.reshape(-1, BLK, kv_weight.shape[1])
    tables = tuple(t.reshape(-1) for t in tables)
    return fused(tables, bias.reshape(-1), tokens[0], queries[0], weight)[None]


def solution(mesh):
    fine = Mesh(mesh.devices.reshape(4, 4, 2, 4), ("x", "z", "c", "y"))
    ctx = ("x", "z", "c")
    return jax.shard_map(
        on_device,
        mesh=fine,
        in_specs=(P("y", ctx, None), P("y", ctx, None), P(None, "y"), P(), P()),
        out_specs=P("y", ctx, None),
        check_vma=False,
    )
```

time: 852 us -> 191 us (0.22); the launches traced: 840 us -> 191 us
  local copies, waits for them, and re-layouts: 279 us -> 8.03 us
  Pallas kernels: 0 us -> 181 us
  other arithmetic: 175 us -> 1.64 us
  waiting for transfers between devices: 167 us -> 0 us
  matrix products: 97.9 us -> 0 us
  blocking collectives: 80.7 us -> 0 us
  starting transfers between devices: 21.3 us -> 0 us
  between operations: 13.7 us -> 0.04 us
    pallas_call x0 -> x1, Pallas kernels: none -> 181 us  [fused(): pl.pallas_call(fused_kernel, out_shape=jax.ShapeDtypeStruct(queries.shape...]
    all_gather x1 -> x0, waiting for transfers between devices: 157 us -> none  [on_device(): lax.all_gather(tokens, 'fsdp', axis=0, tiled=True)]
    unnamed x3 -> x0, other arithmetic: 131 us -> none
    unnamed x15 -> x1, local copies, waits for them, and re-layouts: 115 us -> 4.64 us
    dot_general x15 -> x0, matrix products: 97.9 us -> none  [the longest x7 71 us: slot_step(): jnp.einsum('nqhk,nkd->nqhd', weights.astype(jnp.bfloat16), value_rows, pr...]
    all_to_all x1 -> x0, blocking collectives: 80.7 us -> none  [on_device(): lax.all_to_all(result, 'ctx', split_axis=1, concat_axis=2, tiled=True)]
    broadcast_in_dim x5 -> x0, local copies, waits for them, and re-layouts: 54.3 us -> none  [the longest x2 50 us: on_device(): jnp.broadcast_to(keyvals.reshape(1, seq_rows, kv_heads, 1, pair_width), (...]
    reshape x3, local copies, waits for them, and re-layouts: 39.4 us -> 2.28 us  [on_device(): tables = tuple((t.reshape(-1) for t in tables))]
  transfers between devices with their start and end apart: 4 -> 0, of which waited for: 2 -> 0; matrix products, arithmetic and copies ran while one was open for 25% -> 0% of each run, Pallas kernels for 0% -> 0%
where the time goes in v1:
time: 191 us
  Pallas kernels  181 us (95%)
  local copies, waits for them, and re-layouts  8.03 us (4%)
    pallas_call x1, Pallas kernels, fused(): pl.pallas_call(fused_kernel, out_shape=jax.ShapeDtypeStruct(queries.shape...  181 us
    unnamed x1, local copies, waits for them, and re-layouts  4.64 us

profile of v1, /device:TPU:24, one launch (start us, length us, event | category | flops | bytes accessed | tf_op | source)
XLA Modules:
  0.0 191.1 jit_solution(12995196442806875643)
XLA Ops:
  0.0 0.8 add_select_fusion
  0.8 0.1 copy.8
  1.0 0.8 reshape.22.third
  1.7 0.1 copy.6
  1.8 0.8 reshape.20.first
  2.6 0.1 copy.7
  2.7 0.8 reshape.21.second
  3.5 0.8 fusion
  4.3 0.7 select_n.47.bias
  5.1 181.4 %fused.1 = bf16[256,8192]{1,0:T(8,128)(2,1)} custom-call(s32[4096]{0:T(1024)} %reshape.20.first, s32[4096]{0:T(1024)} %reshape.21.second, s32[4096]{0:T(1024)} %reshape.22.third, f32[4096]{0:T(1024)} %select_n.47.bias, bf16[256,8192]{1,0:T(8,128)(2,1)} %bitcast.6, bf16[256,8192]{1,0:T(8,128)(2,1)} %bitcast.7, bf16[64,128,512]{2,1,0:T(8,128)(2,1)} %bitcast.5), custom_call_target="tpu_custom_call" | custom-call | tf_op jit(solution)/shard_map/fused/pallas_call | solution.py:258
  186.5 4.6 %copy.10 = bf16[1,256,8192]{2,1,0:T(8,128)(2,1)} copy(bf16[1,256,8192]{2,1,0:T(8,128)(2,1)} %bitcast.4) | data formatting | bytes 8388608
